TPU v7x, 256 devices: a whole 4x4x8 slice. The times are simulated.
256 devices in a mesh: feat: 4 (over y), rows: 64 (over x, z, core).
Axes of the slice: x: 4, y: 4, z: 8, core: 2. Of those that a mesh axis runs over, the one named last changes fastest.
Arguments:
- features: bfloat16 [16384, 4096], P('rows', 'feat'), may hold values from -16 to 16
- labels: int32 [16384], P('rows'), may hold values from 0 to 639
- inv_gram: float32 [4, 1024, 1024], P('feat'), may hold values from -1 to 1, as said below
Outputs:
- weights: float32 [4096, 640], P(('feat', 'rows'))
- after_block: float32 [4, 16384, 640], P('feat', 'rows')
Inputs may be any that keep to these rules, and one draw needn't show every extreme that they name: Each of the 4 matrices of inv_gram is symmetric.
All inputs are finite; a program needn't handle non-finite values.
Results may differ from a plain program's by a relative error of at most 0.0094.
Values sent between devices are 32-bit elements; how exact they have to be, the bound alone decides.
No kernel may reach another device: no remote copies, remote signals or barrier semaphores. Data moves between devices by JAX's collectives and lax.ppermute only.
A program may use at most 64 MiB of HBM per device.

v0:
```python
import jax
import jax.numpy as jnp
from jax import lax
from jax.sharding import PartitionSpec as P

C = 640
CLS_BLK = 128


def shifted(value, axis, by):
    count = lax.axis_size(axis)
    pairs = [(i, i + by) for i in range(count) if 0 <= i + by < count]
    return lax.ppermute(value, axis, pairs)


def local(features, labels, inv_gram):
    rows_here = features.shape[0]
    block_width = features.shape[1]
    group_total = lax.axis_size("feat")
    shard_total = lax.axis_size("rows")
    feat_index = lax.axis_index("feat")
    shard_index = lax.axis_index("rows")
    row_share = block_width // shard_total
    class_block = CLS_BLK
    wave_total = C // class_block
    class_ids = jnp.arange(C, dtype=jnp.int32)
    onehot = (labels[:, None] == class_ids[None, :]).astype(jnp.float32)
    counts = lax.psum(jnp.sum(onehot, axis=0), "rows")
    count_row = jnp.sum(onehot * counts[None, :], axis=1)
    row_weight = float(rows_here * shard_total) / (C * count_row)
    inverse = inv_gram[0]
    residual = jnp.where(feat_index == 0, onehot, jnp.zeros_like(onehot))
    solved_all = jnp.zeros((row_share, C), jnp.float32)
    own_first = shard_index * row_share
    for segment in range(group_total + wave_total - 1):
        wave_index = segment - feat_index
        active = (wave_index >= 0) & (wave_index < wave_total)
        column_start = jnp.clip(wave_index, 0, wave_total - 1) * class_block
        current = lax.dynamic_slice_in_dim(residual, column_start, class_block, 1)
        scaled = (row_weight[:, None] * current).astype(jnp.bfloat16)
        partial_value = lax.dot_general(
            features, scaled, (((0,), (0,)), ((), ())), preferred_element_type=jnp.float32
        )
        summed = lax.psum(partial_value, "rows")
        solved = jnp.dot(
            inverse, summed, precision=lax.Precision.HIGHEST, preferred_element_type=jnp.float32
        )
        correction = jnp.dot(
            features, solved.astype(jnp.bfloat16), preferred_element_type=jnp.float32
        )
        new_rows = lax.dynamic_slice_in_dim(solved, own_first, row_share, 0)
        updated = current - correction
        residual = jnp.where(
            active, lax.dynamic_update_slice_in_dim(residual, updated, column_start, 1), residual
        )
        solved_all = jnp.where(
            active,
            lax.dynamic_update_slice_in_dim(solved_all, new_rows, column_start, 1),
            solved_all,
        )
        arrived = shifted(updated, "feat", 1)
        incoming = segment - feat_index + 1
        landing = (feat_index >= 1) & (incoming >= 0) & (incoming < wave_total)
        landing_start = jnp.clip(incoming, 0, wave_total - 1) * class_block
        residual = jnp.where(
            landing, lax.dynamic_update_slice_in_dim(residual, arrived, landing_start, 1), residual
        )
    return (solved_all, residual[None])


def solution(mesh):
    in_specs = (P("rows", "feat"), P("rows"), P("feat", None, None))
    out_specs = (P(("feat", "rows"), None), P("feat", "rows", None))
    return jax.shard_map(local, mesh=mesh, in_specs=in_specs, out_specs=out_specs, check_vma=False)
```

profile of v0, /device:TPU:8, one launch (start us, length us, event | category | flops | bytes accessed | tf_op | source)
XLA Modules:
  0.0 1711.2 jit_solution(7271068267111447395)
XLA Ops:
  7.2 0.9 convert_reduce_fusion
  8.1 131.5 %psum.63 = f32[640]{0:T(1024)S(1)} all-reduce(f32[640]{0:T(1024)S(1)} %convert_reduce_fusion), channel_id=1, replica_groups=mesh['feat'=4,'rows'=64] {'rows'}, use_global_device_ids=true, to_apply=%region_1.0 | all-reduce | flops 640 | bytes 5120 | tf_op jit(solution)/shard_map/psum | solution.py:28
  139.7 0.9 select_reduce_fusion
  140.6 1.0 convolution_bitcast_fusion.7
  141.7 177.3 %all-reduce.9.cloned.1.call-done = f32[1024,128]{0,1:T(8,128)} async-done(((f32[1024,128]{0,1:T(8,128)}), f32[1024,128]{0,1:T(8,128)}) %all-reduce.9.cloned.1.call-update) | async-done | bytes 524304 | tf_op jit(solution)/shard_map/psum | solution.py:44
  319.0 6.7 fusion.14
  325.8 0.3 fusion.23
  326.1 3.4 collective-permute-start
  329.5 3.4 collective-permute-done
  333.0 1.0 convolution_bitcast_fusion.6
  334.1 180.6 %all-reduce.11.cloned.1.call-done = f32[1024,128]{0,1:T(8,128)} async-done(((f32[1024,128]{0,1:T(8,128)}), f32[1024,128]{0,1:T(8,128)}) %all-reduce.11.cloned.1.call-update) | async-done | bytes 524304 | tf_op jit(solution)/shard_map/psum | solution.py:44
  514.7 6.7 fusion.12
  521.4 0.3 fusion.22
  521.8 3.4 collective-permute-start.1
  525.2 3.4 collective-permute-done.1
  528.6 1.0 convolution_bitcast_fusion.5
  529.7 0.2 all-reduce.15.cloned.1.call-start
  529.9 180.4 %all-reduce.13.cloned.1.call-done = f32[1024,128]{0,1:T(8,128)} async-done(((f32[1024,128]{0,1:T(8,128)}), f32[1024,128]{0,1:T(8,128)}) %all-reduce.13.cloned.1.call-update) | async-done | bytes 524304 | tf_op jit(solution)/shard_map/psum | solution.py:44
  710.3 6.7 fusion.10
  717.1 0.3 fusion.21
  717.4 3.4 collective-permute-start.2
  720.8 3.4 collective-permute-done.2
  724.3 1.0 convolution_bitcast_fusion.4
  725.4 180.6 %all-reduce.15.cloned.1.call-done = f32[1024,128]{0,1:T(8,128)} async-done(((f32[1024,128]{0,1:T(8,128)}), f32[1024,128]{0,1:T(8,128)}) %all-reduce.15.cloned.1.call-update) | async-done | bytes 524304 | tf_op jit(solution)/shard_map/psum | solution.py:44
  905.9 6.7 fusion.8
  912.7 0.3 fusion.20
  913.0 3.4 collective-permute-start.3
  916.5 3.4 collective-permute-done.3
  919.9 1.0 convolution_bitcast_fusion.3
  921.0 180.5 %all-reduce.17.cloned.1.call-done = f32[1024,128]{0,1:T(8,128)} async-done(((f32[1024,128]{0,1:T(8,128)}), f32[1024,128]{0,1:T(8,128)}) %all-reduce.17.cloned.1.call-update) | async-done | bytes 524304 | tf_op jit(solution)/shard_map/psum | solution.py:44
  1101.6 6.7 fusion.6
  1108.3 0.3 fusion.19
  1108.7 3.4 collective-permute-start.4
  1112.1 3.4 collective-permute-done.4
  1115.6 1.1 convolution_bitcast_fusion.2
  1116.6 0.3 all-reduce.21.cloned.1.call-start
  1117.0 0.1 bitcast_dynamic-update-slice_fusion.1
  1117.1 180.2 %all-reduce.19.cloned.1.call-done = f32[1024,128]{0,1:T(8,128)} async-done(((f32[1024,128]{0,1:T(8,128)}), f32[1024,128]{0,1:T(8,128)}) %all-reduce.19.cloned.1.call-update) | async-done | bytes 524304 | tf_op jit(solution)/shard_map/psum | solution.py:44
  1297.2 6.7 fusion.4
  1304.0 0.3 fusion.18
  1304.3 3.4 collective-permute-start.5
  1307.8 3.4 collective-permute-done.5
  1311.2 1.1 convolution_bitcast_fusion.1
  1312.3 0.0 all-reduce.23.cloned.1.call-start
  1312.3 0.1 fusion.38
  1312.4 0.1 fusion.37
  1312.5 0.9 fusion.36
  1313.5 179.4 %all-reduce.21.cloned.1.call-done = f32[1024,128]{0,1:T(8,128)} async-done(((f32[1024,128]{0,1:T(8,128)}), f32[1024,128]{0,1:T(8,128)}) %all-reduce.21.cloned.1.call-update) | async-done | bytes 524304 | tf_op jit(solution)/shard_map/psum | solution.py:44
  1492.9 6.7 fusion.2
  1499.6 0.3 fusion.17
  1499.9 3.4 collective-permute-start.6
  1503.4 3.4 collective-permute-done.6
  1506.8 1.0 convolution_bitcast_fusion
  1507.9 0.9 fusion.35
  1508.8 0.1 fusion.34
  1508.9 0.1 fusion.33
  1509.0 179.5 %all-reduce.23.cloned.1.call-done = f32[1024,128]{0,1:T(8,128)} async-done(((f32[1024,128]{0,1:T(8,128)}), f32[1024,128]{0,1:T(8,128)}) %all-reduce.23.cloned.1.call-update) | async-done | bytes 524304 | tf_op jit(solution)/shard_map/psum | solution.py:44
  1688.5 6.7 fusion
  1695.2 0.3 fusion.16
  1695.6 0.1 fusion.32
  1695.7 0.8 copy.5
  1696.4 3.4 collective-permute-start.7
  1699.9 3.4 collective-permute-done.7
  1703.3 1.1 copy.6
  (38 shorter events, 0.8 us)
Async XLA Ops:
  7.2 133.4 %copy-start = (bf16[256,1024]{1,0:T(8,128)(2,1)S(1)}, bf16[256,1024]{1,0:T(8,128)(2,1)}, u32[]{:S(2)}) copy-start(bf16[256,1024]{1,0:T(8,128)(2,1)} %param.3) | copy-start | bytes 1572868
  7.2 311.9 %all-reduce.9.cloned.1.call-start = ((), (), s32[]{:S(2)}) async-start(), calls=%async_computation | async-start | bytes 1048576 | tf_op jit(solution)/shard_map/psum | solution.py:44
  141.6 373.0 %all-reduce.11.cloned.1.call-start = ((), (), s32[]{:S(2)}) async-start(), calls=%async_computation.1 | async-start | bytes 1048576 | tf_op jit(solution)/shard_map/psum | solution.py:44
  326.1 6.9 collective-permute-start
  334.0 376.3 %all-reduce.13.cloned.1.call-start = ((), (), s32[]{:S(2)}) async-start(), calls=%async_computation.2 | async-start | bytes 1048576 | tf_op jit(solution)/shard_map/psum | solution.py:44
  521.8 6.9 collective-permute-start.1
  529.7 376.2 %all-reduce.15.cloned.1.call-start = ((), (), s32[]{:S(2)}) async-start(), calls=%async_computation.3 | async-start | bytes 1048576 | tf_op jit(solution)/shard_map/psum | solution.py:44
  717.4 6.9 collective-permute-start.2
  725.3 376.3 %all-reduce.17.cloned.1.call-start = ((), (), s32[]{:S(2)}) async-start(), calls=%async_computation.4 | async-start | bytes 1048576 | tf_op jit(solution)/shard_map/psum | solution.py:44
  912.7 7.2 copy-start.1
  913.0 6.9 collective-permute-start.3
  921.0 376.3 %all-reduce.19.cloned.1.call-start = ((), (), s32[]{:S(2)}) async-start(), calls=%async_computation.5 | async-start | bytes 1048576 | tf_op jit(solution)/shard_map/psum | solution.py:44
  1108.3 7.2 copy-start.2
  1108.7 6.9 collective-permute-start.4
  1116.6 376.2 %all-reduce.21.cloned.1.call-start = ((), (), s32[]{:S(2)}) async-start(), calls=%async_computation.6 | async-start | bytes 1048576 | tf_op jit(solution)/shard_map/psum | solution.py:44
  1304.3 6.9 collective-permute-start.5
  1312.3 376.2 %all-reduce.23.cloned.1.call-start = ((), (), s32[]{:S(2)}) async-start(), calls=%async_computation.7 | async-start | bytes 1048576 | tf_op jit(solution)/shard_map/psum | solution.py:44
  1499.9 6.9 collective-permute-start.6
  1696.4 6.8 collective-permute-start.7
Sparse Core Ops, SparseCore 0:
  141.8 177.2 all-reduce.8
  334.2 180.4 all-reduce.10
  529.8 180.4 all-reduce.12
  725.4 180.4 all-reduce.14
  921.1 180.4 all-reduce.16
  1116.8 180.4 all-reduce.18
  1312.4 180.4 all-reduce.20
  1508.0 180.4 all-reduce.22
where the time goes:
time: 1710 us
  waiting for transfers between devices  1470 us (86%)
  blocking collectives  132 us (8%)
  matrix products  64.7 us (4%)
  starting transfers between devices  27.9 us (2%)
    psum x8, waiting for transfers between devices, local(): summed = lax.psum(partial_value, 'rows')  1440 us
    psum x1, blocking collectives, local(): counts = lax.psum(jnp.sum(onehot, axis=0), 'rows')  132 us
    dot_general x8, matrix products, local(): jnp.dot(inverse, summed, precision=lax.Precision.HIGHEST, preferred_eleme...  53.9 us
  transfers between devices with their start and end apart: 16, of which 16 were waited for; matrix products, arithmetic and copies ran while one was open for 0% of the time, Pallas kernels for 0%

commit v1 on v0

--- a/solution.py
+++ b/solution.py
@@ -25,7 +25,9 @@
     wave_total = C // class_block
     class_ids = jnp.arange(C, dtype=jnp.int32)
     onehot = (labels[:, None] == class_ids[None, :]).astype(jnp.float32)
-    counts = lax.psum(jnp.sum(onehot, axis=0), "rows")
+    part = jnp.sum(onehot, axis=0)
+    parts = lax.all_gather(part, "rows")
+    counts = jnp.sum(parts, axis=0)
     count_row = jnp.sum(onehot * counts[None, :], axis=1)
     row_weight = float(rows_here * shard_total) / (C * count_row)
     inverse = inv_gram[0]

time: 1710 us -> 1630 us (0.953)
  blocking collectives: 132 us -> 47.2 us
    psum x1 -> x0, blocking collectives: 132 us -> none  [local(): counts = lax.psum(jnp.sum(onehot, axis=0), 'rows')]
    all_gather x0 -> x1, blocking collectives: none -> 47.2 us  [local(): parts = lax.all_gather(part, 'rows')]
where the time goes in v1:
time: 1630 us
  waiting for transfers between devices  1470 us (90%)
  matrix products  64.7 us (4%)
  blocking collectives  47.2 us (3%)
  starting transfers between devices  27.9 us (2%)
    psum x8, waiting for transfers between devices, local(): summed = lax.psum(partial_value, 'rows')  1440 us
    dot_general x8, matrix products, local(): jnp.dot(inverse, summed, precision=lax.Precision.HIGHEST, preferred_eleme...  53.9 us
    all_gather x1, blocking collectives, local(): parts = lax.all_gather(part, 'rows')  47.2 us
  transfers between devices with their start and end apart: 16, of which 16 were waited for; matrix products, arithmetic and copies ran while one was open for 0% of the time, Pallas kernels for 0%

profile of v1, /device:TPU:8, one launch (start us, length us, event | category | flops | bytes accessed | tf_op | source)
XLA Modules:
  0.0 1630.6 jit_solution(12035348842562350987)
XLA Ops:
  7.2 0.9 convert_reduce_fusion
  8.1 47.2 %all-gather.1 = f32[64,1,640]{2,1,0:T(1,128)S(1)} all-gather(f32[1,1,640]{2,1,0:T(1,128)S(1)} %reshape.13), channel_id=2, replica_groups=mesh['feat'=4,'rows'=64] {'rows'}, dimensions={0}, use_global_device_ids=true | all-gather | bytes 166400 | tf_op jit(solution)/shard_map/all_gather | solution.py:29
  55.3 0.1 reduce_sum.28
  55.4 0.9 select_reduce_fusion
  56.3 1.0 convolution_bitcast_fusion.7
  57.5 181.0 %all-reduce.9.cloned.1.call-done = f32[1024,128]{0,1:T(8,128)} async-done(((f32[1024,128]{0,1:T(8,128)}), f32[1024,128]{0,1:T(8,128)}) %all-reduce.9.cloned.1.call-update) | async-done | bytes 524304 | tf_op jit(solution)/shard_map/psum | solution.py:46
  238.5 6.7 fusion.14
  245.2 0.3 fusion.23
  245.5 3.4 collective-permute-start
  249.0 3.4 collective-permute-done
  252.4 1.0 convolution_bitcast_fusion.6
  253.5 180.5 %all-reduce.11.cloned.1.call-done = f32[1024,128]{0,1:T(8,128)} async-done(((f32[1024,128]{0,1:T(8,128)}), f32[1024,128]{0,1:T(8,128)}) %all-reduce.11.cloned.1.call-update) | async-done | bytes 524304 | tf_op jit(solution)/shard_map/psum | solution.py:46
  434.1 6.7 fusion.12
  440.8 0.3 fusion.22
  441.1 3.4 collective-permute-start.1
  444.6 3.4 collective-permute-done.1
  448.0 1.0 convolution_bitcast_fusion.5
  449.1 0.2 all-reduce.15.cloned.1.call-start
  449.3 180.4 %all-reduce.13.cloned.1.call-done = f32[1024,128]{0,1:T(8,128)} async-done(((f32[1024,128]{0,1:T(8,128)}), f32[1024,128]{0,1:T(8,128)}) %all-reduce.13.cloned.1.call-update) | async-done | bytes 524304 | tf_op jit(solution)/shard_map/psum | solution.py:46
  629.7 6.7 fusion.10
  636.4 0.3 fusion.21
  636.8 3.4 collective-permute-start.2
  640.2 3.4 collective-permute-done.2
  643.6 1.0 convolution_bitcast_fusion.4
  644.8 180.6 %all-reduce.15.cloned.1.call-done = f32[1024,128]{0,1:T(8,128)} async-done(((f32[1024,128]{0,1:T(8,128)}), f32[1024,128]{0,1:T(8,128)}) %all-reduce.15.cloned.1.call-update) | async-done | bytes 524304 | tf_op jit(solution)/shard_map/psum | solution.py:46
  825.3 6.7 fusion.8
  832.1 0.3 fusion.20
  832.4 3.4 collective-permute-start.3
  835.9 3.4 collective-permute-done.3
  839.3 1.0 convolution_bitcast_fusion.3
  840.4 180.5 %all-reduce.17.cloned.1.call-done = f32[1024,128]{0,1:T(8,128)} async-done(((f32[1024,128]{0,1:T(8,128)}), f32[1024,128]{0,1:T(8,128)}) %all-reduce.17.cloned.1.call-update) | async-done | bytes 524304 | tf_op jit(solution)/shard_map/psum | solution.py:46
  1021.0 6.7 fusion.6
  1027.7 0.3 fusion.19
  1028.1 3.4 collective-permute-start.4
  1031.5 3.4 collective-permute-done.4
  1035.0 1.1 convolution_bitcast_fusion.2
  1036.0 0.3 all-reduce.21.cloned.1.call-start
  1036.4 0.1 bitcast_dynamic-update-slice_fusion.1
  1036.5 180.2 %all-reduce.19.cloned.1.call-done = f32[1024,128]{0,1:T(8,128)} async-done(((f32[1024,128]{0,1:T(8,128)}), f32[1024,128]{0,1:T(8,128)}) %all-reduce.19.cloned.1.call-update) | async-done | bytes 524304 | tf_op jit(solution)/shard_map/psum | solution.py:46
  1216.6 6.7 fusion.4
  1223.4 0.3 fusion.18
  1223.7 3.4 collective-permute-start.5
  1227.1 3.4 collective-permute-done.5
  1230.6 1.1 convolution_bitcast_fusion.1
  1231.7 0.1 fusion.38
  1231.8 0.1 fusion.37
  1231.9 0.9 fusion.36
  1232.8 179.4 %all-reduce.21.cloned.1.call-done = f32[1024,128]{0,1:T(8,128)} async-done(((f32[1024,128]{0,1:T(8,128)}), f32[1024,128]{0,1:T(8,128)}) %all-reduce.21.cloned.1.call-update) | async-done | bytes 524304 | tf_op jit(solution)/shard_map/psum | solution.py:46
  1412.3 6.7 fusion.2
  1419.0 0.3 fusion.17
  1419.3 3.4 collective-permute-start.6
  1422.8 3.4 collective-permute-done.6
  1426.2 1.0 convolution_bitcast_fusion
  1427.3 0.9 fusion.35
  1428.2 0.1 fusion.34
  1428.3 0.1 fusion.33
  1428.4 179.5 %all-reduce.23.cloned.1.call-done = f32[1024,128]{0,1:T(8,128)} async-done(((f32[1024,128]{0,1:T(8,128)}), f32[1024,128]{0,1:T(8,128)}) %all-reduce.23.cloned.1.call-update) | async-done | bytes 524304 | tf_op jit(solution)/shard_map/psum | solution.py:46
  1607.9 6.7 fusion
  1614.6 0.3 fusion.16
  1615.0 0.1 fusion.32
  1615.1 0.8 copy.7
  1615.8 3.4 collective-permute-start.7
  1619.3 3.4 collective-permute-done.7
  1622.7 1.1 copy.8
  (40 shorter events, 0.8 us)
Async XLA Ops:
  7.2 49.2 %copy-start = (bf16[256,1024]{1,0:T(8,128)(2,1)S(1)}, bf16[256,1024]{1,0:T(8,128)(2,1)}, u32[]{:S(2)}) copy-start(bf16[256,1024]{1,0:T(8,128)(2,1)} %param.3) | copy-start | bytes 1572868
  7.2 231.3 %all-reduce.9.cloned.1.call-start = ((), (), s32[]{:S(2)}) async-start(), calls=%async_computation | async-start | bytes 1048576 | tf_op jit(solution)/shard_map/psum | solution.py:46
  57.4 376.7 %all-reduce.11.cloned.1.call-start = ((), (), s32[]{:S(2)}) async-start(), calls=%async_computation.1 | async-start | bytes 1048576 | tf_op jit(solution)/shard_map/psum | solution.py:46
  245.5 6.9 collective-permute-start
  253.5 376.2 %all-reduce.13.cloned.1.call-start = ((), (), s32[]{:S(2)}) async-start(), calls=%async_computation.2 | async-start | bytes 1048576 | tf_op jit(solution)/shard_map/psum | solution.py:46
  441.1 6.9 collective-permute-start.1
  449.1 376.2 %all-reduce.15.cloned.1.call-start = ((), (), s32[]{:S(2)}) async-start(), calls=%async_computation.3 | async-start | bytes 1048576 | tf_op jit(solution)/shard_map/psum | solution.py:46
  636.8 6.9 collective-permute-start.2
  644.7 376.3 %all-reduce.17.cloned.1.call-start = ((), (), s32[]{:S(2)}) async-start(), calls=%async_computation.4 | async-start | bytes 1048576 | tf_op jit(solution)/shard_map/psum | solution.py:46
  832.1 7.2 copy-start.1
  832.4 6.9 collective-permute-start.3
  840.4 376.3 %all-reduce.19.cloned.1.call-start = ((), (), s32[]{:S(2)}) async-start(), calls=%async_computation.5 | async-start | bytes 1048576 | tf_op jit(solution)/shard_map/psum | solution.py:46
  1027.7 7.2 copy-start.2
  1028.1 6.9 collective-permute-start.4
  1036.0 376.2 %all-reduce.21.cloned.1.call-start = ((), (), s32[]{:S(2)}) async-start(), calls=%async_computation.6 | async-start | bytes 1048576 | tf_op jit(solution)/shard_map/psum | solution.py:46
  1223.7 6.9 collective-permute-start.5
  1231.7 376.2 %all-reduce.23.cloned.1.call-start = ((), (), s32[]{:S(2)}) async-start(), calls=%async_computation.7 | async-start | bytes 1048576 | tf_op jit(solution)/shard_map/psum | solution.py:46
  1419.3 6.9 collective-permute-start.6
  1615.8 6.8 collective-permute-start.7
Sparse Core Ops, SparseCore 0:
  57.5 180.8 all-reduce.8
  253.6 180.4 all-reduce.10
  449.2 180.4 all-reduce.12
  644.8 180.4 all-reduce.14
  840.5 180.4 all-reduce.16
  1036.1 180.4 all-reduce.18
  1231.8 180.4 all-reduce.20
  1427.4 180.4 all-reduce.22
